TPU v7x, 512 devices: a whole 4x8x8 slice. The times are simulated.
512 devices in a mesh: pole: 16 (over x, z_lo, core), slab: 32 (over y, z_hi).
Axes of the slice: x: 4, y: 8, z: 8 (z_hi: 4, z_lo: 2; z = z_hi * 2 + z_lo), core: 2. Of those that a mesh axis runs over, the one named last changes fastest.
Arguments:
- vectors: float32 [2, 16, 128, 16, 128], P(None, None, 'slab'), may hold values from -6 to 6
- potential: float32 [128, 16, 128], P('slab'), may hold values from 0 to 2
Outputs:
- filtered: float32 [2, 16, 128, 16, 128], P(None, None, 'slab', 'pole')
- gram_correlation: float32 [2, 16, 16], replicated
- gram_energy: float32 [2, 16, 16], replicated
All inputs are finite; a program needn't handle non-finite values.
Results may differ from a plain program's by a relative error of at most 0.005.
Values sent between devices are 32-bit elements; how exact they have to be, the bound alone decides.
No kernel may reach another device: no remote copies, remote signals or barrier semaphores. Data moves between devices by JAX's collectives and lax.ppermute only.
A program may use at most 64 MiB of HBM per device.

v0:
```python
import math
import jax
import jax.numpy as jnp
from jax import lax
from jax.sharding import PartitionSpec as P

ITERS = 3
contour_center = 2.0
contour_radius = 1.5


def extended(block, sides, width):
    for axis, dim in sides:
        count = lax.axis_size(axis)
        forward = [(i, i + 1) for i in range(count - 1)]
        forward.append((count - 1, 0))
        backward = [(target, source) for source, target in forward]
        low = lax.ppermute(
            lax.slice_in_dim(block, block.shape[dim] - width, None, axis=dim), axis, forward
        )
        high = lax.ppermute(lax.slice_in_dim(block, 0, width, axis=dim), axis, backward)
        block = jnp.concatenate([low, block, high], axis=dim)
    return block


def apply_shifted(block, potential, shift_re, shift_im):
    padded = extended(block, (("slab", 2),), 1)
    beside = padded[:, :, 2:] + padded[:, :, :-2]
    beside = beside + jnp.roll(block, 1, 3) + jnp.roll(block, -1, 3)
    beside = beside + jnp.roll(block, 1, 4) + jnp.roll(block, -1, 4)
    diagonal = shift_re - 3.0 - potential
    real_part = diagonal * block[0] - shift_im * block[1] + 0.5 * beside[0]
    imag_part = diagonal * block[1] + shift_im * block[0] + 0.5 * beside[1]
    return jnp.stack([real_part, imag_part])


def bilinear(left, right):
    real_part = jnp.sum(left[0] * right[0] - left[1] * right[1], axis=(1, 2, 3))
    imag_part = jnp.sum(left[0] * right[1] + left[1] * right[0], axis=(1, 2, 3))
    return jnp.stack([real_part, imag_part])


def complex_divide(numer, denom):
    magnitude = denom[0] * denom[0] + denom[1] * denom[1]
    return jnp.stack(
        [
            (numer[0] * denom[0] + numer[1] * denom[1]) / magnitude,
            (numer[1] * denom[0] - numer[0] * denom[1]) / magnitude,
        ]
    )


def column_scale(coef, block):
    first = coef[0][:, None, None, None]
    second = coef[1][:, None, None, None]
    return jnp.stack([first * block[0] - second * block[1], first * block[1] + second * block[0]])


def scalar_scale(first, second, block):
    return jnp.stack([first * block[0] - second * block[1], first * block[1] + second * block[0]])


def inner(left, right):
    return lax.dot_general(
        left,
        right,
        (((1,), (1,)), ((), ())),
        precision=lax.Precision.HIGHEST,
        preferred_element_type=jnp.float32,
    )


def gram_pair(filtered, image, cells):
    count = filtered.shape[1]
    sre = filtered[0].reshape(count, -1)
    sim = filtered[1].reshape(count, -1)
    hre = image[0].reshape(count, -1)
    him = image[1].reshape(count, -1)
    correlation = (
        jnp.stack([inner(sre, sre) + inner(sim, sim), inner(sre, sim) - inner(sim, sre)]) / cells
    )
    energy = (
        jnp.stack([inner(sre, hre) + inner(sim, him), inner(sre, him) - inner(sim, hre)]) / cells
    )
    return (correlation, energy)


def residual_form(residual):
    return lax.psum(bilinear(residual, residual), "slab")


def on_device(vectors, potential):
    pole_count = lax.axis_size("pole")
    angle = 2.0 * math.pi / pole_count * (lax.axis_index("pole").astype(jnp.float32) + 0.5)
    cosine = jnp.cos(angle)
    sine = jnp.sin(angle)
    shift_re = contour_center + contour_radius * cosine
    shift_im = contour_radius * sine
    weight_re = contour_radius * cosine / pole_count
    weight_im = contour_radius * sine / pole_count
    solution = jnp.zeros_like(vectors)
    residual = vectors
    direction = vectors
    rho = residual_form(residual)
    for iteration in range(ITERS):
        mapped = apply_shifted(direction, potential, shift_re, shift_im)
        curve = lax.psum(bilinear(direction, mapped), "slab")
        alpha = complex_divide(rho, curve)
        solution = solution + column_scale(alpha, direction)
        residual = residual - column_scale(alpha, mapped)
        if iteration + 1 < ITERS:
            rho_new = residual_form(residual)
            direction = residual + column_scale(complex_divide(rho_new, rho), direction)
            rho = rho_new
    weighted = scalar_scale(weight_re, weight_im, solution)
    hsol = scalar_scale(shift_re, shift_im, solution) - vectors + residual
    weighted_image = scalar_scale(weight_re, weight_im, hsol)
    cells = vectors.shape[2] * lax.axis_size("slab") * vectors.shape[3] * vectors.shape[4]
    filtered, image = lax.psum((weighted, weighted_image), "pole")
    correlation, energy = gram_pair(filtered, image, cells)
    correlation, energy = lax.psum((correlation, energy), "slab")
    rows = filtered.shape[3] // pole_count
    own = lax.dynamic_slice_in_dim(filtered, lax.axis_index("pole") * rows, rows, 3)
    return (own, correlation, energy)


def solution(mesh):
    in_specs = (P(None, None, "slab", None, None), P("slab", None, None))
    out_specs = (P(None, None, "slab", "pole", None), P(), P())
    return jax.shard_map(
        on_device, mesh=mesh, in_specs=in_specs, out_specs=out_specs, check_vma=False
    )
```

profile of v0, /device:TPU:32, one launch (start us, length us, event | category | flops | bytes accessed | tf_op | source)
XLA Modules:
  0.0 801.4 jit_solution(13384978102229270736)
XLA Ops:
  7.2 1.8 copy.5
  9.1 10.8 %collective-permute-start = (f32[2,16,1,16,128]{4,1,3,2,0:T(8,128)S(1)}, f32[2,16,1,16,128]{4,1,3,2,0:T(8,128)S(1)}, u32[]{:S(2)}, u32[]{:S(2)}) collective-permute-start(f32[2,16,1,16,128]{4,1,3,2,0:T(8,128)S(1)} %get-tuple-element.77), channel_id=1, source_target_pairs={{1,0},{2,1},{3,2},{4,3},{5,4},{6,5},{7,6},{8,7},{9,8},{10,9},{11,1... | collective-permute-start | bytes 786440 | tf_op jit(solution)/shard_map/ppermute | solution.py:21
  19.9 1.9 collective-permute-start.1
  21.9 1.5 fusion.68
  23.3 1.6 fusion.67
  25.0 1.7 fusion.66
  26.8 2.0 collective-permute-done
  28.8 10.6 %collective-permute-done.1 = f32[2,16,1,16,128]{4,1,3,2,0:T(8,128)S(1)} collective-permute-done((f32[2,16,1,16,128]{4,1,3,2,0:T(8,128)S(1)}, f32[2,16,1,16,128]{4,1,3,2,0:T(8,128)S(1)}, u32[]{:S(2)}, u32[]{:S(2)}) %collective-permute-start.1) | collective-permute-done | bytes 262176 | tf_op jit(solution)/shard_map/ppermute | solution.py:18
  39.4 3.4 fusion.22
  43.5 76.9 %all-reduce.1 = (f32[2,16]{1,0:T(2,128)S(1)}, f32[2,16]{1,0:T(2,128)S(1)}) all-reduce(f32[2,16]{1,0:T(2,128)S(1)} %get-tuple-element.90, f32[2,16]{1,0:T(2,128)S(1)} %get-tuple-element.89), channel_id=1, replica_groups=mesh['pole'=16,'slab'=32] {'slab'}, use_global_device_ids=true, to_apply=%region_5.6 | all-reduce | flops 64 | bytes 512 | tf_op jit(solution)/shard_map/psum | solution.py:107
  120.4 1.4 multiply_subtract_fusion.9
  121.9 1.1 copy-done
  123.9 79.8 %psum.72 = f32[2,16]{1,0:T(2,128)S(1)} all-reduce(f32[2,16]{1,0:T(2,128)S(1)} %pad_maximum_fusion.10), channel_id=1, replica_groups=mesh['pole'=16,'slab'=32] {'slab'}, use_global_device_ids=true, to_apply=%region_8.9 | all-reduce | flops 32 | bytes 256 | tf_op jit(solution)/shard_map/psum | solution.py:89
  205.3 3.2 collective-permute-start.2
  208.6 3.5 collective-permute-start.3
  212.3 4.7 collective-permute-done.2
  217.0 6.9 collective-permute-done.3
  225.6 76.8 %psum.73 = f32[2,16]{1,0:T(2,128)S(1)} all-reduce(f32[2,16]{1,0:T(2,128)S(1)} %pad_maximum_fusion.11), channel_id=1, replica_groups=mesh['pole'=16,'slab'=32] {'slab'}, use_global_device_ids=true, to_apply=%region_11.12 | all-reduce | flops 32 | bytes 256 | tf_op jit(solution)/shard_map/psum | solution.py:107
  302.5 2.5 multiply_subtract_fusion.6
  306.8 79.9 %psum.74 = f32[2,16]{1,0:T(2,128)S(1)} all-reduce(f32[2,16]{1,0:T(2,128)S(1)} %pad_maximum_fusion.12), channel_id=1, replica_groups=mesh['pole'=16,'slab'=32] {'slab'}, use_global_device_ids=true, to_apply=%region_14.15 | all-reduce | flops 32 | bytes 256 | tf_op jit(solution)/shard_map/psum | solution.py:89
  389.5 2.9 collective-permute-start.4
  392.4 4.0 collective-permute-start.5
  396.7 4.3 collective-permute-done.4
  401.0 6.6 collective-permute-done.5
  409.3 76.8 %psum.75 = f32[2,16]{1,0:T(2,128)S(1)} all-reduce(f32[2,16]{1,0:T(2,128)S(1)} %pad_maximum_fusion.13), channel_id=1, replica_groups=mesh['pole'=16,'slab'=32] {'slab'}, use_global_device_ids=true, to_apply=%region_17.18 | all-reduce | flops 32 | bytes 256 | tf_op jit(solution)/shard_map/psum | solution.py:107
  486.2 1.6 multiply_subtract_fusion.1
  491.6 1.0 pad_maximum_fusion.7
  492.7 1.1 pad_maximum_fusion.6
  493.8 134.6 %all-reduce.5.cloned.1.call-done = (f32[2,16,4,16,128]{4,1,3,2,0:T(8,128)}, f32[2,16,4,16,128]{4,1,3,2,0:T(8,128)}) async-done(((f32[2,16,4,16,128]{4,1,3,2,0:T(8,128)}, f32[2,16,4,16,128]{4,1,3,2,0:T(8,128)}), (f32[2,16,4,16,128]{4,1,3,2,0:T(8,128)}, f32[2,16,4,16,128]{4,1,3,2,0:T(8,128)})) %all-reduce.5.cloned.1.call-update) | async-done | bytes 2097168 | tf_op jit(solution)/shard_map/psum | solution.py:119
  628.5 2.1 convolution_bitcast_fusion
  630.5 1.8 convolution_bitcast_fusion.2
  638.0 156.6 %all-reduce = (f32[2,16,16]{2,1,0:T(8,128)}, f32[2,16,16]{2,1,0:T(8,128)}) all-reduce(f32[2,16,16]{2,1,0:T(8,128)S(1)} %maximum_multiply_fusion, f32[2,16,16]{2,1,0:T(8,128)S(1)} %maximum_multiply_fusion.1), channel_id=1, replica_groups=mesh['pole'=16,'slab'=32] {'slab'}, use_global_device_ids=true, to_apply=%region_19.20 | all-reduce | flops 1024 | bytes 8192 | tf_op jit(solution)/shard_map/psum | solution.py:121
  (86 shorter events, 21.2 us)
Async XLA Ops:
  7.2 621.3 %all-reduce.5.cloned.1.call-start = ((), (), s32[]{:S(2)}) async-start(), calls=%async_computation | async-start | bytes 4194304 | tf_op jit(solution)/shard_map/psum | solution.py:119
  9.1 19.7 %collective-permute-start = (f32[2,16,1,16,128]{4,1,3,2,0:T(8,128)S(1)}, f32[2,16,1,16,128]{4,1,3,2,0:T(8,128)S(1)}, u32[]{:S(2)}, u32[]{:S(2)}) collective-permute-start(f32[2,16,1,16,128]{4,1,3,2,0:T(8,128)S(1)} %get-tuple-element.77), channel_id=1, source_target_pairs={{1,0},{2,1},{3,2},{4,3},{5,4},{6,5},{7,6},{8,7},{9,8},{10,9},{11,1... | collective-permute-start | bytes 786440 | tf_op jit(solution)/shard_map/ppermute | solution.py:21
  19.9 19.5 %collective-permute-start.1 = (f32[2,16,1,16,128]{4,1,3,2,0:T(8,128)S(1)}, f32[2,16,1,16,128]{4,1,3,2,0:T(8,128)S(1)}, u32[]{:S(2)}, u32[]{:S(2)}) collective-permute-start(f32[2,16,1,16,128]{4,1,3,2,0:T(8,128)S(1)} %get-tuple-element.78), channel_id=1, source_target_pairs={{0,1},{1,2},{2,3},{3,4},{4,5},{5,6},{6,7},{7,8},{8,9},{9,10},{10,1... | collective-permute-start | bytes 786440 | tf_op jit(solution)/shard_map/ppermute | solution.py:18
  25.0 1.8 copy-start.15
  121.8 1.2 copy-start
  205.3 11.6 %collective-permute-start.2 = (f32[2,16,1,16,128]{4,1,3,2,0:T(8,128)S(1)}, f32[2,16,1,16,128]{4,1,3,2,0:T(8,128)S(1)}, u32[]{:S(2)}, u32[]{:S(2)}) collective-permute-start(f32[2,16,1,16,128]{4,1,3,2,0:T(8,128)S(1)} %get-tuple-element.67), channel_id=1, source_target_pairs={{1,0},{2,1},{3,2},{4,3},{5,4},{6,5},{7,6},{8,7},{9,8},{10,9},{11,1... | collective-permute-start | bytes 786440 | tf_op jit(solution)/shard_map/ppermute | solution.py:21
  208.6 15.3 %collective-permute-start.3 = (f32[2,16,1,16,128]{4,1,3,2,0:T(8,128)S(1)}, f32[2,16,1,16,128]{4,1,3,2,0:T(8,128)S(1)}, u32[]{:S(2)}, u32[]{:S(2)}) collective-permute-start(f32[2,16,1,16,128]{4,1,3,2,0:T(8,128)S(1)} %get-tuple-element.68), channel_id=1, source_target_pairs={{0,1},{1,2},{2,3},{3,4},{4,5},{5,6},{6,7},{7,8},{8,9},{9,10},{10,1... | collective-permute-start | bytes 786440 | tf_op jit(solution)/shard_map/ppermute | solution.py:18
  224.6 1.0 copy-start.3
  305.0 0.8 copy-start.7
  305.1 1.4 copy-start.4
  386.7 1.0 copy-start.5
  386.7 1.2 copy-start.8
  389.5 11.5 %collective-permute-start.4 = (f32[2,16,1,16,128]{4,1,3,2,0:T(8,128)S(1)}, f32[2,16,1,16,128]{4,1,3,2,0:T(8,128)S(1)}, u32[]{:S(2)}, u32[]{:S(2)}) collective-permute-start(f32[2,16,1,16,128]{4,1,3,2,0:T(8,128)S(1)} %get-tuple-element.57), channel_id=1, source_target_pairs={{1,0},{2,1},{3,2},{4,3},{5,4},{6,5},{7,6},{8,7},{9,8},{10,9},{11,1... | collective-permute-start | bytes 786440 | tf_op jit(solution)/shard_map/ppermute | solution.py:21
  392.4 15.2 %collective-permute-start.5 = (f32[2,16,1,16,128]{4,1,3,2,0:T(8,128)S(1)}, f32[2,16,1,16,128]{4,1,3,2,0:T(8,128)S(1)}, u32[]{:S(2)}, u32[]{:S(2)}) collective-permute-start(f32[2,16,1,16,128]{4,1,3,2,0:T(8,128)S(1)} %get-tuple-element.58), channel_id=1, source_target_pairs={{0,1},{1,2},{2,3},{3,4},{4,5},{5,6},{6,7},{7,8},{8,9},{9,10},{10,1... | collective-permute-start | bytes 786440 | tf_op jit(solution)/shard_map/ppermute | solution.py:18
  408.3 1.0 copy-start.2
  486.2 1.8 copy-start.14
  487.8 1.0 copy-start.11
  487.8 1.2 copy-start.12
  487.8 1.3 copy-start.13
  489.3 1.0 copy-start.6
  489.4 1.2 copy-start.9
  628.5 2.1 copy-start.1
  632.3 1.6 copy-start.10
Sparse Core Ops, SparseCore 0:
  493.9 134.4 all-reduce.4
where the time goes:
time: 802 us; the launch traced here: 801 us
  blocking collectives  547 us (68%)
  waiting for transfers between devices  170 us (21%)
  starting transfers between devices  26.4 us (3%)
  other arithmetic  20.1 us (3%)
  local copies, waits for them, and re-layouts  15 us (2%)
  between operations  14.6 us (2%)
  matrix products  8.76 us (1%)
    psum x3, blocking collectives, on_device(): curve = lax.psum(bilinear(direction, mapped), 'slab')  231 us
    psum x2, blocking collectives, residual_form(): return lax.psum(bilinear(residual, residual), 'slab')  160 us
    psum x1, blocking collectives, on_device(): correlation, energy = lax.psum((correlation, energy), 'slab')  157 us
    psum x1, waiting for transfers between devices, on_device(): filtered, image = lax.psum((weighted, weighted_image), 'pole')  135 us
    ppermute x3, waiting for transfers between devices, extended(): lax.ppermute(lax.slice_in_dim(block, block.shape[dim] - width, None, axis...  24.2 us
    ppermute x3, starting transfers between devices, extended(): lax.ppermute(lax.slice_in_dim(block, 0, width, axis=dim), axis, backward)  17 us
  transfers between devices with their start and end apart: 7, of which 7 were waited for; matrix products, arithmetic and copies ran while one was open for 1% of the time, Pallas kernels for 0%

commit v1 on v0

--- a/solution.py
+++ b/solution.py
@@ -86,7 +86,7 @@
 
 
 def residual_form(residual):
-    return lax.psum(bilinear(residual, residual), "slab")
+    return jnp.sum(lax.all_gather(bilinear(residual, residual), "slab"), axis=0)
 
 
 def on_device(vectors, potential):

time: 802 us -> 878 us (1.095)
  blocking collectives: 547 us -> 624 us
    all_gather x0 -> x3, blocking collectives: none -> 237 us  [residual_form(): return jnp.sum(lax.all_gather(bilinear(residual, residual), 'slab'), axis=0)]
    psum x2 -> x0, blocking collectives: 160 us -> none  [residual_form(): return lax.psum(bilinear(residual, residual), 'slab')]
where the time goes in v1:
time: 878 us; the launch traced here: 877 us
  blocking collectives  624 us (71%)
  waiting for transfers between devices  168 us (19%)
  starting transfers between devices  26.4 us (3%)
  other arithmetic  20 us (2%)
  local copies, waits for them, and re-layouts  15 us (2%)
  between operations  14.6 us (2%)
    all_gather x3, blocking collectives, residual_form(): return jnp.sum(lax.all_gather(bilinear(residual, residual), 'slab'), axis=0)  237 us
    psum x3, blocking collectives, on_device(): curve = lax.psum(bilinear(direction, mapped), 'slab')  231 us
    psum x1, blocking collectives, on_device(): correlation, energy = lax.psum((correlation, energy), 'slab')  157 us
    psum x1, waiting for transfers between devices, on_device(): filtered, image = lax.psum((weighted, weighted_image), 'pole')  135 us
    ppermute x3, waiting for transfers between devices, extended(): lax.ppermute(lax.slice_in_dim(block, block.shape[dim] - width, None, axis...  21 us
  transfers between devices with their start and end apart: 7, of which 7 were waited for; matrix products, arithmetic and copies ran while one was open for 1% of the time, Pallas kernels for 0%

profile of v1, /device:TPU:32, one launch (start us, length us, event | category | flops | bytes accessed | tf_op | source)
XLA Modules:
  0.0 876.9 jit_solution(12837067556677013388)
XLA Ops:
  7.2 1.8 copy.22
  9.1 10.8 %collective-permute-start = (f32[2,16,1,16,128]{4,1,3,2,0:T(8,128)S(1)}, f32[2,16,1,16,128]{4,1,3,2,0:T(8,128)S(1)}, u32[]{:S(2)}, u32[]{:S(2)}) collective-permute-start(f32[2,16,1,16,128]{4,1,3,2,0:T(8,128)S(1)} %get-tuple-element.78), channel_id=1, source_target_pairs={{1,0},{2,1},{3,2},{4,3},{5,4},{6,5},{7,6},{8,7},{9,8},{10,9},{11,1... | collective-permute-start | bytes 786440 | tf_op jit(solution)/shard_map/ppermute | solution.py:21
  19.9 1.9 collective-permute-start.1
  21.9 1.4 fusion.68
  23.3 1.6 fusion.67
  24.9 1.7 fusion.66
  26.8 2.0 collective-permute-done
  28.8 10.6 %collective-permute-done.1 = f32[2,16,1,16,128]{4,1,3,2,0:T(8,128)S(1)} collective-permute-done((f32[2,16,1,16,128]{4,1,3,2,0:T(8,128)S(1)}, f32[2,16,1,16,128]{4,1,3,2,0:T(8,128)S(1)}, u32[]{:S(2)}, u32[]{:S(2)}) %collective-permute-start.1) | collective-permute-done | bytes 262176 | tf_op jit(solution)/shard_map/ppermute | solution.py:18
  39.4 3.4 fusion.22
  43.5 76.9 %psum.49 = f32[2,16]{1,0:T(2,128)S(1)} all-reduce(f32[2,16]{1,0:T(2,128)S(1)} %pad_maximum_fusion.8), channel_id=1, replica_groups=mesh['pole'=16,'slab'=32] {'slab'}, use_global_device_ids=true, to_apply=%region_5.6 | all-reduce | flops 32 | bytes 256 | tf_op jit(solution)/shard_map/psum | solution.py:107
  120.4 78.2 %all-gather.3 = f32[32,2,16]{2,1,0:T(2,128)S(1)} all-gather(f32[1,2,16]{2,1,0:T(2,128)S(1)} %maximum_bitcast_fusion), channel_id=2, replica_groups=mesh['pole'=16,'slab'=32] {'slab'}, dimensions={0}, use_global_device_ids=true | all-gather | bytes 4224 | tf_op jit(solution)/shard_map/all_gather | solution.py:89
  198.6 1.4 multiply_subtract_fusion.9
  200.1 1.1 copy-done
  202.1 78.7 %all-gather.4 = f32[32,2,16]{2,1,0:T(2,128)S(1)} all-gather(f32[1,2,16]{2,1,0:T(2,128)S(1)} %maximum_bitcast_fusion.1), channel_id=3, replica_groups=mesh['pole'=16,'slab'=32] {'slab'}, dimensions={0}, use_global_device_ids=true | all-gather | bytes 4224 | tf_op jit(solution)/shard_map/all_gather | solution.py:89
  282.6 1.9 collective-permute-start.2
  284.5 4.8 collective-permute-start.3
  289.5 5.5 collective-permute-done.2
  295.0 5.2 collective-permute-done.3
  301.9 76.8 %psum.50 = f32[2,16]{1,0:T(2,128)S(1)} all-reduce(f32[2,16]{1,0:T(2,128)S(1)} %pad_maximum_fusion.9), channel_id=1, replica_groups=mesh['pole'=16,'slab'=32] {'slab'}, use_global_device_ids=true, to_apply=%region_11.12 | all-reduce | flops 32 | bytes 256 | tf_op jit(solution)/shard_map/psum | solution.py:107
  378.7 2.5 multiply_subtract_fusion.6
  383.1 80.1 %all-gather.5 = f32[32,2,16]{2,1,0:T(2,128)S(1)} all-gather(f32[1,2,16]{2,1,0:T(2,128)S(1)} %maximum_bitcast_fusion.2), channel_id=4, replica_groups=mesh['pole'=16,'slab'=32] {'slab'}, dimensions={0}, use_global_device_ids=true | all-gather | bytes 4224 | tf_op jit(solution)/shard_map/all_gather | solution.py:89
  466.1 1.9 collective-permute-start.4
  468.0 5.0 collective-permute-start.5
  473.2 4.8 collective-permute-done.4
  478.1 5.2 collective-permute-done.5
  484.9 76.8 %psum.51 = f32[2,16]{1,0:T(2,128)S(1)} all-reduce(f32[2,16]{1,0:T(2,128)S(1)} %pad_maximum_fusion.10), channel_id=1, replica_groups=mesh['pole'=16,'slab'=32] {'slab'}, use_global_device_ids=true, to_apply=%region_17.18 | all-reduce | flops 32 | bytes 256 | tf_op jit(solution)/shard_map/psum | solution.py:107
  561.8 1.6 multiply_subtract_fusion.1
  566.2 1.8 pad_maximum_fusion.6
  569.2 134.8 %all-reduce.4.cloned.1.call-done = (f32[2,16,4,16,128]{4,1,3,2,0:T(8,128)}, f32[2,16,4,16,128]{4,1,3,2,0:T(8,128)}) async-done(((f32[2,16,4,16,128]{4,1,3,2,0:T(8,128)}, f32[2,16,4,16,128]{4,1,3,2,0:T(8,128)}), (f32[2,16,4,16,128]{4,1,3,2,0:T(8,128)}, f32[2,16,4,16,128]{4,1,3,2,0:T(8,128)})) %all-reduce.4.cloned.1.call-update) | async-done | bytes 2097168 | tf_op jit(solution)/shard_map/psum | solution.py:119
  704.0 2.1 convolution_bitcast_fusion
  706.0 1.8 convolution_bitcast_fusion.2
  713.5 156.6 %all-reduce = (f32[2,16,16]{2,1,0:T(8,128)}, f32[2,16,16]{2,1,0:T(8,128)}) all-reduce(f32[2,16,16]{2,1,0:T(8,128)S(1)} %maximum_multiply_fusion, f32[2,16,16]{2,1,0:T(8,128)S(1)} %maximum_multiply_fusion.1), channel_id=1, replica_groups=mesh['pole'=16,'slab'=32] {'slab'}, use_global_device_ids=true, to_apply=%region_19.20 | all-reduce | flops 1024 | bytes 8192 | tf_op jit(solution)/shard_map/psum | solution.py:121
  (90 shorter events, 21.4 us)
Async XLA Ops:
  7.2 696.8 %all-reduce.4.cloned.1.call-start = ((), (), s32[]{:S(2)}) async-start(), calls=%async_computation | async-start | bytes 4194304 | tf_op jit(solution)/shard_map/psum | solution.py:119
  9.1 19.7 %collective-permute-start = (f32[2,16,1,16,128]{4,1,3,2,0:T(8,128)S(1)}, f32[2,16,1,16,128]{4,1,3,2,0:T(8,128)S(1)}, u32[]{:S(2)}, u32[]{:S(2)}) collective-permute-start(f32[2,16,1,16,128]{4,1,3,2,0:T(8,128)S(1)} %get-tuple-element.78), channel_id=1, source_target_pairs={{1,0},{2,1},{3,2},{4,3},{5,4},{6,5},{7,6},{8,7},{9,8},{10,9},{11,1... | collective-permute-start | bytes 786440 | tf_op jit(solution)/shard_map/ppermute | solution.py:21
  19.9 19.5 %collective-permute-start.1 = (f32[2,16,1,16,128]{4,1,3,2,0:T(8,128)S(1)}, f32[2,16,1,16,128]{4,1,3,2,0:T(8,128)S(1)}, u32[]{:S(2)}, u32[]{:S(2)}) collective-permute-start(f32[2,16,1,16,128]{4,1,3,2,0:T(8,128)S(1)} %get-tuple-element.79), channel_id=1, source_target_pairs={{0,1},{1,2},{2,3},{3,4},{4,5},{5,6},{6,7},{7,8},{8,9},{9,10},{10,1... | collective-permute-start | bytes 786440 | tf_op jit(solution)/shard_map/ppermute | solution.py:18
  24.9 1.8 copy-start.15
  200.0 1.2 copy-start
  282.6 12.5 %collective-permute-start.2 = (f32[2,16,1,16,128]{4,1,3,2,0:T(8,128)S(1)}, f32[2,16,1,16,128]{4,1,3,2,0:T(8,128)S(1)}, u32[]{:S(2)}, u32[]{:S(2)}) collective-permute-start(f32[2,16,1,16,128]{4,1,3,2,0:T(8,128)S(1)} %get-tuple-element.68), channel_id=1, source_target_pairs={{1,0},{2,1},{3,2},{4,3},{5,4},{6,5},{7,6},{8,7},{9,8},{10,9},{11,1... | collective-permute-start | bytes 786440 | tf_op jit(solution)/shard_map/ppermute | solution.py:21
  284.5 15.7 %collective-permute-start.3 = (f32[2,16,1,16,128]{4,1,3,2,0:T(8,128)S(1)}, f32[2,16,1,16,128]{4,1,3,2,0:T(8,128)S(1)}, u32[]{:S(2)}, u32[]{:S(2)}) collective-permute-start(f32[2,16,1,16,128]{4,1,3,2,0:T(8,128)S(1)} %get-tuple-element.69), channel_id=1, source_target_pairs={{0,1},{1,2},{2,3},{3,4},{4,5},{5,6},{6,7},{7,8},{8,9},{9,10},{10,1... | collective-permute-start | bytes 786440 | tf_op jit(solution)/shard_map/ppermute | solution.py:18
  300.9 1.0 copy-start.3
  381.3 0.8 copy-start.7
  381.4 1.4 copy-start.4
  463.3 1.0 copy-start.5
  463.3 1.2 copy-start.8
  466.1 12.0 %collective-permute-start.4 = (f32[2,16,1,16,128]{4,1,3,2,0:T(8,128)S(1)}, f32[2,16,1,16,128]{4,1,3,2,0:T(8,128)S(1)}, u32[]{:S(2)}, u32[]{:S(2)}) collective-permute-start(f32[2,16,1,16,128]{4,1,3,2,0:T(8,128)S(1)} %get-tuple-element.58), channel_id=1, source_target_pairs={{1,0},{2,1},{3,2},{4,3},{5,4},{6,5},{7,6},{8,7},{9,8},{10,9},{11,1... | collective-permute-start | bytes 786440 | tf_op jit(solution)/shard_map/ppermute | solution.py:21
  468.0 15.2 %collective-permute-start.5 = (f32[2,16,1,16,128]{4,1,3,2,0:T(8,128)S(1)}, f32[2,16,1,16,128]{4,1,3,2,0:T(8,128)S(1)}, u32[]{:S(2)}, u32[]{:S(2)}) collective-permute-start(f32[2,16,1,16,128]{4,1,3,2,0:T(8,128)S(1)} %get-tuple-element.59), channel_id=1, source_target_pairs={{0,1},{1,2},{2,3},{3,4},{4,5},{5,6},{6,7},{7,8},{8,9},{9,10},{10,1... | collective-permute-start | bytes 786440 | tf_op jit(solution)/shard_map/ppermute | solution.py:18
  484.0 1.0 copy-start.2
  561.8 1.8 copy-start.14
  563.4 1.0 copy-start.11
  563.4 1.2 copy-start.12
  563.4 1.3 copy-start.13
  565.0 1.0 copy-start.6
  565.0 1.2 copy-start.9
  704.0 2.1 copy-start.1
  707.8 1.6 copy-start.10
Sparse Core Ops, SparseCore 0:
  569.3 134.5 all-reduce.3
